TPU v7x, 256 devices: a whole 4x4x8 slice. The times are simulated.
256 devices in a mesh: dp: 4 (over x), blk: 16 (over z_lo, y, core), mp: 4 (over z_hi).
Axes of the slice: x: 4, y: 4, z: 8 (z_hi: 4, z_lo: 2; z = z_hi * 2 + z_lo), core: 2. Of those that a mesh axis runs over, the one named last changes fastest.
Arguments:
- tokens: bfloat16 [16384, 7168], P('dp', ('blk', 'mp')), may hold values from -6 to 6
- trainer_q: float32 [3584, 7168], P(('mp', 'blk'), 'dp'), may hold values from -0.0625 to 0.0625
- kv_pool: bfloat16 [2, 8192, 3584], P(None, ('dp', 'blk'), 'mp')
- prompt_kv: bfloat16 [2, 16384, 3584], P(None, ('dp', 'blk'), 'mp'), may hold values from -15 to 15
- page_table: int32 [64, 64], P(('dp', 'blk')), may hold values from 0 to 127, as said below
- page_count: int32 [64], P(('dp', 'blk')), may hold values from 1 to 64
- prompt_len: int32 [64], P(('dp', 'blk')), may hold values from 64 to 256
Outputs:
- server_q: bfloat16 [3584, 7168], P('mp', 'blk')
- attn_out: bfloat16 [16384, 3584], P(('dp', 'blk'), 'mp')
Inputs may be any that keep to these rules, and one draw needn't show every extreme that they name: `page_table`: the entries of a row are distinct page numbers of the request's group.
All inputs are finite; a program needn't handle non-finite values.
Results may differ from a plain program's by a relative error of at most 0.012.
The roundings to bfloat16 on the way count: a program that leaves them out, or rounds other values in their place, can miss the bound.
Values may be sent and summed in bfloat16 or wider, within the bound.
A program may use at most 128 MiB of HBM per device.

v0:
```python
import jax
import jax.numpy as jnp
from jax import lax
from jax.sharding import PartitionSpec as P

HD = 224
PAGE = 16


def attend_block(softmax_state, query_heads, key_heads, value_heads, key_mask):
    running_max, row_total, weighted = softmax_state
    scores = jnp.einsum(
        "thd,khd->htk", query_heads, key_heads, preferred_element_type=jnp.float32
    ) * HD ** (-0.5)
    scores = jnp.where(key_mask[None], scores, -1e30)
    new_max = jnp.maximum(running_max, jnp.max(scores, axis=2))
    weights = jnp.where(key_mask[None], jnp.exp(scores - new_max[:, :, None]), 0.0)
    factor = jnp.exp(running_max - new_max)
    row_total = row_total * factor + jnp.sum(weights, axis=2)
    weighted = weighted * factor[:, :, None] + jnp.einsum(
        "htk,khd->htd",
        weights.astype(jnp.bfloat16),
        value_heads,
        preferred_element_type=jnp.float32,
    )
    return (new_max, row_total, weighted)


def body(tokens, trainer_q, kv_pool, prompt_kv, page_table, page_count, prompt_len):
    blk_size = lax.axis_size("blk")
    mp_size = lax.axis_size("mp")
    dp_size = lax.axis_size("dp")
    g = lax.axis_index("dp")
    own_piece = trainer_q.astype(jnp.bfloat16)
    received = jnp.stack(
        [own_piece]
        + [
            lax.ppermute(own_piece, "dp", [(i, (i + j) % dp_size) for i in range(dp_size)])
            for j in range(1, dp_size)
        ]
    )
    ordered = jnp.take(received, (g - jnp.arange(dp_size)) % dp_size, axis=0)
    trainer_rows = jnp.transpose(ordered, (1, 0, 2)).reshape(own_piece.shape[0], -1)
    head_weights = lax.all_gather(trainer_rows, "blk", axis=0, tiled=True)
    head_width, model_width = head_weights.shape
    block_cols = model_width // blk_size
    server_q = lax.dynamic_slice_in_dim(
        head_weights, lax.axis_index("blk") * block_cols, block_cols, axis=1
    )
    group_rows, piece_cols = tokens.shape
    own_rows = group_rows // blk_size
    pieces = tokens.reshape(blk_size, 1, own_rows, piece_cols)
    pieces = jnp.broadcast_to(pieces, (blk_size, mp_size, own_rows, piece_cols))
    pieces = pieces.reshape(blk_size * mp_size, own_rows, piece_cols)
    pieces = lax.all_to_all(pieces, ("blk", "mp"), 0, 0, tiled=True)
    token_local = jnp.transpose(pieces, (1, 0, 2)).reshape(own_rows, -1)
    queries = jnp.einsum("td,hd->th", token_local, head_weights, preferred_element_type=jnp.float32)
    queries = queries.astype(jnp.bfloat16)
    head_count = head_width // HD
    query_heads = queries.reshape(own_rows, head_count, HD)
    length = prompt_len[0]
    row_pages = page_table[0]
    live_slots = jnp.arange(row_pages.shape[0], dtype=jnp.int32) < page_count[0]
    row_index = jnp.arange(own_rows, dtype=jnp.int32)
    own_mask = (row_index[None, :] <= row_index[:, None]) & (row_index[None, :] < length)
    softmax_state = (
        jnp.full((head_count, own_rows), -1e30, jnp.float32),
        jnp.zeros((head_count, own_rows), jnp.float32),
        jnp.zeros((head_count, own_rows, HD), jnp.float32),
    )
    softmax_state = attend_block(
        softmax_state,
        query_heads,
        prompt_kv[0].reshape(own_rows, head_count, HD),
        prompt_kv[1].reshape(own_rows, head_count, HD),
        own_mask,
    )
    shard_piece = lax.all_gather(kv_pool, "blk", axis=1, tiled=True)
    key_count = shard_piece.shape[1]
    page_ids = jnp.arange(key_count, dtype=jnp.int32) // PAGE
    page_used = jnp.any((row_pages[None, :] == page_ids[:, None]) & live_slots[None, :], axis=1)
    key_mask = jnp.broadcast_to(page_used[None, :], (own_rows, key_count))
    running_max, row_total, weighted = attend_block(
        softmax_state,
        query_heads,
        shard_piece[0].reshape(key_count, head_count, HD),
        shard_piece[1].reshape(key_count, head_count, HD),
        key_mask,
    )
    mixed = weighted / row_total[:, :, None]
    mixed = jnp.where((row_index < length)[None, :, None], mixed, 0.0)
    mixed = jnp.transpose(mixed, (1, 0, 2)).reshape(own_rows, head_width).astype(jnp.bfloat16)
    return (server_q, mixed)


def solution(mesh):
    in_specs = (
        P("dp", ("blk", "mp")),
        P(("mp", "blk"), "dp"),
        P(None, ("dp", "blk"), "mp"),
        P(None, ("dp", "blk"), "mp"),
        P(("dp", "blk"), None),
        P(("dp", "blk")),
        P(("dp", "blk")),
    )
    out_specs = (P("mp", "blk"), P(("dp", "blk"), "mp"))
    return jax.shard_map(body, mesh=mesh, in_specs=in_specs, out_specs=out_specs, check_vma=False)
```

profile of v0, /device:TPU:1, one launch (start us, length us, event | category | flops | bytes accessed | tf_op | source)
XLA Modules:
  0.0 230.1 jit_solution(18045067984531203395)
XLA Ops:
  7.2 0.0 copy-start.2
  7.2 0.0 all-gather.5.cloned.1.call-start
  7.2 0.7 all-gather.5.cloned.1.call-update
  7.9 0.0 all-gather.3.cloned.1.call-start
  8.0 1.0 convert_element_type.21
  9.0 3.4 %collective-permute-start.2 = (bf16[56,1792]{1,0:T(8,128)(2,1)S(1)}, bf16[56,1792]{1,0:T(8,128)(2,1)S(1)}, u32[]{:S(2)}, u32[]{:S(2)}) collective-permute-start(bf16[56,1792]{1,0:T(8,128)(2,1)S(1)} %convert_element_type.21), channel_id=1, source_target_pairs={{0,192},{64,0},{128,64},{192,128},{1,193},{65,1},{129,65},{193,129... | collective-permute-start | bytes 602120 | tf_op jit(solution)/shard_map/ppermute | solution.py:38
  12.4 0.5 collective-permute-start.1
  12.9 0.6 collective-permute-start
  13.5 1.0 convert_bitcast_fusion
  14.6 3.7 %collective-permute-done.2 = bf16[56,1792]{1,0:T(8,128)(2,1)S(1)} collective-permute-done((bf16[56,1792]{1,0:T(8,128)(2,1)S(1)}, bf16[56,1792]{1,0:T(8,128)(2,1)S(1)}, u32[]{:S(2)}, u32[]{:S(2)}) %collective-permute-start.2) | collective-permute-done | bytes 200736 | tf_op jit(solution)/shard_map/ppermute | solution.py:38
  18.2 1.2 collective-permute-done.1
  19.5 5.6 %collective-permute-done = bf16[56,1792]{1,0:T(8,128)(2,1)S(1)} collective-permute-done((bf16[56,1792]{1,0:T(8,128)(2,1)S(1)}, bf16[56,1792]{1,0:T(8,128)(2,1)S(1)}, u32[]{:S(2)}, u32[]{:S(2)}) %collective-permute-start) | collective-permute-done | bytes 200736 | tf_op jit(solution)/shard_map/ppermute | solution.py:38
  25.1 0.1 pad_maximum_fusion
  25.2 0.6 gather_fusion
  25.8 0.1 select_bitcast_fusion
  25.9 0.0 copy-start.3
  26.0 0.9 copy.45
  26.9 0.0 all-gather.3.cloned.1.call-update
  26.9 0.0 copy-done.2
  26.9 0.0 copy-start.4
  27.0 0.1 copy.47
  27.0 2.2 broadcast_in_dim.94
  29.2 12.3 %all-to-all-start = ((bf16[64,256,112]{1,2,0:T(8,128)(2,1)}), bf16[64,256,112]{1,2,0:T(8,128)(2,1)}, u32[]{:S(2)}, u32[]{:S(2)}) async-start(bf16[64,256,112]{1,2,0:T(8,128)(2,1)} %bitcast.77), calls=%async_computation | async-start | bytes 7340032 | tf_op jit(solution)/shard_map/all_to_all | solution.py:55
  42.2 0.0 copy-done.3
  42.2 0.1 fusion.40
  42.3 0.2 copy.36
  43.1 0.2 copy.37
  43.4 0.0 copy-done.4
  43.4 0.2 and_reduce_fusion
  43.6 0.1 fusion.22
  43.7 66.8 %all-gather.5.cloned.1.call-done = bf16[2,2048,896]{2,1,0:T(8,128)(2,1)} async-done(((bf16[2,128,896]{2,1,0:T(8,128)(2,1)}), bf16[2,2048,896]{2,1,0:T(8,128)(2,1)}) %all-gather.5.cloned.1.call-update) | async-done | bytes 7340048 | tf_op jit(solution)/shard_map/all_gather | solution.py:78
  110.5 6.7 %fusion.39 = (bf16[1,2048,896]{2,1,0:T(8,128)(2,1)}, bf16[1,2048,896]{2,1,0:T(8,128)(2,1)}) fusion(bf16[2,2048,896]{2,1,0:T(8,128)(2,1)} %all-gather.5.cloned.1.call-done), kind=kLoop, calls=%fused_computation.68 | loop fusion | bytes 14680064 | tf_op jit(solution)/shard_map/slice | solution.py:86
  117.2 6.2 %copy.40 = bf16[1,2048,896]{1,2,0:T(8,128)(2,1)} copy(bf16[1,2048,896]{2,1,0:T(8,128)(2,1)} %get-tuple-element.13) | data formatting | bytes 7340032 | tf_op jit(solution)/shard_map/slice | solution.py:87
  123.4 6.2 %copy.39 = bf16[1,2048,896]{1,2,0:T(8,128)(2,1)} copy(bf16[1,2048,896]{2,1,0:T(8,128)(2,1)} %get-tuple-element.12) | data formatting | bytes 7340032 | tf_op jit(solution)/shard_map/slice | solution.py:86
  129.6 73.3 %all-gather.3.cloned.1.call-done = bf16[896,7168]{1,0:T(8,128)(2,1)} async-done(((bf16[56,7168]{1,0:T(8,128)(2,1)}), bf16[896,7168]{1,0:T(8,128)(2,1)}) %all-gather.3.cloned.1.call-update) | async-done | bytes 12845072 | tf_op jit(solution)/shard_map/all_gather | solution.py:44
  202.8 1.6 constant_dynamic-slice_fusion
  204.5 1.2 copy.41
  205.7 0.0 all-to-all-done
  205.7 0.0 copy-start
  205.7 9.3 %convolution_convert_fusion = bf16[896,256]{1,0:T(8,128)(2,1)S(1)} fusion(bf16[896,7168]{1,0:T(8,128)(2,1)} %all-gather.3.cloned.1.call-done, bf16[256,7168]{0,1:T(8,128)(2,1)} %bitcast.9), kind=kOutput, calls=%fused_computation.17 | convolution fusion | flops 3288563712 | bytes 16973824 | tf_op jit(solution)/shard_map/td,hd->th/dot_general | solution.py:57
  215.0 0.0 copy-done
  215.0 0.0 copy-start.1
  215.1 1.9 fusion
  216.9 0.4 fusion.41
  217.3 2.2 fusion.1
  219.5 0.0 copy-done.1
  219.5 2.1 fusion.7
  221.7 0.2 fusion.16
  221.9 0.4 fusion.15
  222.3 1.0 copy.42
  (8 shorter events, 0.1 us)
Async XLA Ops:
  7.2 19.8 %copy-start.2 = (bf16[4096,112]{0,1:T(8,128)(2,1)S(1)}, bf16[4096,112]{0,1:T(8,128)(2,1)}, u32[]{:S(2)}) copy-start(bf16[4096,112]{0,1:T(8,128)(2,1)} %param.7) | copy-start | bytes 2752516
  7.2 103.3 %all-gather.5.cloned.1.call-start = ((), (), s32[]{:S(2)}) async-start(), calls=%async_computation.2 | async-start | bytes 7798784 | tf_op jit(solution)/shard_map/all_gather | solution.py:78
  7.9 194.9 %all-gather.3.cloned.1.call-start = ((), (), s32[]{:S(2)}) async-start(), calls=%async_computation.1 | async-start | bytes 13647872 | tf_op jit(solution)/shard_map/all_gather | solution.py:44
  9.0 9.2 %collective-permute-start.2 = (bf16[56,1792]{1,0:T(8,128)(2,1)S(1)}, bf16[56,1792]{1,0:T(8,128)(2,1)S(1)}, u32[]{:S(2)}, u32[]{:S(2)}) collective-permute-start(bf16[56,1792]{1,0:T(8,128)(2,1)S(1)} %convert_element_type.21), channel_id=1, source_target_pairs={{0,192},{64,0},{128,64},{192,128},{1,193},{65,1},{129,65},{193,129... | collective-permute-start | bytes 602120 | tf_op jit(solution)/shard_map/ppermute | solution.py:38
  12.4 7.1 %collective-permute-start.1 = (bf16[56,1792]{1,0:T(8,128)(2,1)S(1)}, bf16[56,1792]{1,0:T(8,128)(2,1)S(1)}, u32[]{:S(2)}, u32[]{:S(2)}) collective-permute-start(bf16[56,1792]{1,0:T(8,128)(2,1)S(1)} %convert_element_type.21), channel_id=1, source_target_pairs={{0,128},{64,192},{128,0},{192,64},{1,129},{65,193},{129,1},{193,65... | collective-permute-start | bytes 602120 | tf_op jit(solution)/shard_map/ppermute | solution.py:38
  12.9 12.2 %collective-permute-start = (bf16[56,1792]{1,0:T(8,128)(2,1)S(1)}, bf16[56,1792]{1,0:T(8,128)(2,1)S(1)}, u32[]{:S(2)}, u32[]{:S(2)}) collective-permute-start(bf16[56,1792]{1,0:T(8,128)(2,1)S(1)} %convert_element_type.21), channel_id=1, source_target_pairs={{0,64},{64,128},{128,192},{192,0},{1,65},{65,129},{129,193},{193,1... | collective-permute-start | bytes 602120 | tf_op jit(solution)/shard_map/ppermute | solution.py:38
  25.9 16.2 %copy-start.3 = (bf16[2,256,896]{2,1,0:T(8,128)(2,1)S(1)}, bf16[2,256,896]{2,1,0:T(8,128)(2,1)}, u32[]{:S(2)}) copy-start(bf16[2,256,896]{2,1,0:T(8,128)(2,1)} %param.10) | copy-start | bytes 2752516
  26.9 16.5 %copy-start.4 = (s32[1,64]{1,0:T(1,128)S(1)}, s32[1,64]{1,0:T(1,128)}, u32[]{:S(2)}) copy-start(s32[1,64]{1,0:T(1,128)} %param.11) | copy-start | bytes 772
  29.2 176.5 %all-to-all-start = ((bf16[64,256,112]{1,2,0:T(8,128)(2,1)}), bf16[64,256,112]{1,2,0:T(8,128)(2,1)}, u32[]{:S(2)}, u32[]{:S(2)}) async-start(bf16[64,256,112]{1,2,0:T(8,128)(2,1)} %bitcast.77), calls=%async_computation | async-start | bytes 7340032 | tf_op jit(solution)/shard_map/all_to_all | solution.py:55
  205.7 9.3 %copy-start = (bf16[1,2048,896]{1,2,0:T(8,128)(2,1)S(1)}, bf16[1,2048,896]{1,2,0:T(8,128)(2,1)}, u32[]{:S(2)}) copy-start(bf16[1,2048,896]{1,2,0:T(8,128)(2,1)} %copy.39) | copy-start | bytes 11010052
  215.0 4.5 %copy-start.1 = (bf16[1,2048,896]{1,2,0:T(8,128)(2,1)S(1)}, bf16[1,2048,896]{1,2,0:T(8,128)(2,1)}, u32[]{:S(2)}) copy-start(bf16[1,2048,896]{1,2,0:T(8,128)(2,1)} %copy.40) | copy-start | bytes 11010052
Sparse Core Ops, SparseCore 0:
  9.8 100.6 all-gather.4
  112.9 89.8 all-gather.2
where the time goes:
time: 231 us; the launch traced here: 230 us
  waiting for transfers between devices  151 us (65%)
  local copies, waits for them, and re-layouts  27.2 us (12%)
  starting transfers between devices  16.9 us (7%)
  between operations  15.6 us (7%)
  matrix products  14.1 us (6%)
  other arithmetic  5.04 us (2%)
    all_gather x1, waiting for transfers between devices, body(): head_weights = lax.all_gather(trainer_rows, 'blk', axis=0, tiled=True)  73.3 us
    all_gather x1, waiting for transfers between devices, body(): shard_piece = lax.all_gather(kv_pool, 'blk', axis=1, tiled=True)  66.8 us
    slice x2, local copies, waits for them, and re-layouts, body(): shard_piece[0].reshape(key_count, head_count, HD)  12.9 us
    all_to_all x1, starting transfers between devices, body(): pieces = lax.all_to_all(pieces, ('blk', 'mp'), 0, 0, tiled=True)  12.3 us
    ppermute x3, waiting for transfers between devices, body(): lax.ppermute(own_piece, 'dp', [(i, (i + j) % dp_size) for i in range(dp_s...  10.5 us
    dot_general x1, matrix products, body(): jnp.einsum('td,hd->th', token_local, head_weights, preferred_element_type...  9.31 us
    slice x1, local copies, waits for them, and re-layouts, body(): shard_piece[1].reshape(key_count, head_count, HD)  6.17 us
  transfers between devices with their start and end apart: 6, of which 5 were waited for; matrix products, arithmetic and copies ran while one was open for 13% of the time, Pallas kernels for 0%

commit v1 on v0

--- a/solution.py
+++ b/solution.py
@@ -41,7 +41,9 @@
     )
     ordered = jnp.take(received, (g - jnp.arange(dp_size)) % dp_size, axis=0)
     trainer_rows = jnp.transpose(ordered, (1, 0, 2)).reshape(own_piece.shape[0], -1)
-    head_weights = lax.all_gather(trainer_rows, "blk", axis=0, tiled=True)
+    head_weights = jnp.concatenate(
+        lax.all_to_all(jnp.stack([trainer_rows] * lax.axis_size("blk")), "blk", 0, 0), axis=0
+    )
     head_width, model_width = head_weights.shape
     block_cols = model_width // blk_size
     server_q = lax.dynamic_slice_in_dim(

time: 231 us -> 346 us (1.50)
  waiting for transfers between devices: 151 us -> 255 us
  starting transfers between devices: 16.9 us -> 22.6 us
  local copies, waits for them, and re-layouts: 27.2 us -> 32.3 us
    all_to_all x0 -> x1, waiting for transfers between devices: none -> 183 us  [body(): lax.all_to_all(jnp.stack([trainer_rows] * lax.axis_size('blk')), 'blk', 0...]
    all_gather x1 -> x0, waiting for transfers between devices: 73.3 us -> none  [body(): head_weights = lax.all_gather(trainer_rows, 'blk', axis=0, tiled=True)]
    all_gather x1, waiting for transfers between devices: 66.8 us -> 0.02 us  [body(): shard_piece = lax.all_gather(kv_pool, 'blk', axis=1, tiled=True)]
    all_to_all x1, waiting for transfers between devices: 0.01 us -> 60.8 us  [body(): pieces = lax.all_to_all(pieces, ('blk', 'mp'), 0, 0, tiled=True)]
    all_to_all x0 -> x1, starting transfers between devices: none -> 6.46 us  [body(): lax.all_to_all(jnp.stack([trainer_rows] * lax.axis_size('blk')), 'blk', 0...]
    another operation x0 -> x2, local copies, waits for them, and re-layouts: none -> 6.26 us  [body(): jnp.stack([trainer_rows] * lax.axis_size('blk'))]
  transfers between devices with their start and end apart: 6 -> 6, of which waited for: 5 -> 5; matrix products, arithmetic and copies ran while one was open for 13% -> 7% of each run, Pallas kernels for 0% -> 0%
where the time goes in v1:
time: 346 us; the launch traced here: 345 us
  waiting for transfers between devices  255 us (74%)
  local copies, waits for them, and re-layouts  32.3 us (9%)
  starting transfers between devices  22.6 us (7%)
  between operations  15.6 us (5%)
  matrix products  14.1 us (4%)
  other arithmetic  5.04 us (1%)
    all_to_all x1, waiting for transfers between devices, body(): lax.all_to_all(jnp.stack([trainer_rows] * lax.axis_size('blk')), 'blk', 0...  183 us
    all_to_all x1, waiting for transfers between devices, body(): pieces = lax.all_to_all(pieces, ('blk', 'mp'), 0, 0, tiled=True)  60.8 us
    slice x2, local copies, waits for them, and re-layouts, body(): shard_piece[0].reshape(key_count, head_count, HD)  12.8 us
    all_to_all x1, starting transfers between devices, body(): pieces = lax.all_to_all(pieces, ('blk', 'mp'), 0, 0, tiled=True)  11.6 us
    ppermute x3, waiting for transfers between devices, body(): lax.ppermute(own_piece, 'dp', [(i, (i + j) % dp_size) for i in range(dp_s...  10.5 us
    dot_general x1, matrix products, body(): jnp.einsum('td,hd->th', token_local, head_weights, preferred_element_type...  9.31 us
  transfers between devices with their start and end apart: 6, of which 5 were waited for; matrix products, arithmetic and copies ran while one was open for 7% of the time, Pallas kernels for 0%

profile of v1, /device:TPU:1, one launch (start us, length us, event | category | flops | bytes accessed | tf_op | source)
XLA Modules:
  0.0 345.0 jit_solution(10040140252083589940)
XLA Ops:
  7.2 1.0 convert_element_type.21
  8.2 3.4 collective-permute-start.2
  11.6 0.5 collective-permute-start.1
  12.1 0.6 collective-permute-start
  12.7 1.0 convert_bitcast_fusion
  13.8 3.7 %collective-permute-done.2 = bf16[56,1792]{1,0:T(8,128)(2,1)S(1)} collective-permute-done((bf16[56,1792]{1,0:T(8,128)(2,1)S(1)}, bf16[56,1792]{1,0:T(8,128)(2,1)S(1)}, u32[]{:S(2)}, u32[]{:S(2)}) %collective-permute-start.2) | collective-permute-done | bytes 200736 | tf_op jit(solution)/shard_map/ppermute | solution.py:38
  17.4 1.2 collective-permute-done.1
  18.7 5.6 %collective-permute-done = bf16[56,1792]{1,0:T(8,128)(2,1)S(1)} collective-permute-done((bf16[56,1792]{1,0:T(8,128)(2,1)S(1)}, bf16[56,1792]{1,0:T(8,128)(2,1)S(1)}, u32[]{:S(2)}, u32[]{:S(2)}) %collective-permute-start) | collective-permute-done | bytes 200736 | tf_op jit(solution)/shard_map/ppermute | solution.py:38
  24.3 0.1 pad_maximum_fusion
  24.4 0.6 gather_fusion
  25.0 0.1 select_bitcast_fusion
  25.2 0.1 copy.36
  25.2 6.2 %stack.23 = bf16[16,56,7168]{2,1,0:T(8,128)(2,1)} broadcast(bf16[56,7168]{1,0:T(8,128)(2,1)S(1)} %bitcast.82), dimensions={1,2} | broadcast | bytes 13647872 | tf_op jit(solution)/shard_map/stack | solution.py:45
  31.4 0.0 copy-start.2
  31.4 6.5 %all-to-all-start = ((bf16[16,56,7168]{2,1,0:T(8,128)(2,1)}), bf16[16,56,7168]{2,1,0:T(8,128)(2,1)}, u32[]{:S(2)}, u32[]{:S(2)}) async-start(bf16[16,56,7168]{2,1,0:T(8,128)(2,1)} %stack.23), calls=%async_computation | async-start | bytes 25690112 | tf_op jit(solution)/shard_map/all_to_all | solution.py:45
  37.9 0.0 copy-start.3
  37.9 0.0 all-gather.2.cloned.1.call-start
  37.9 0.7 all-gather.2.cloned.1.call-update
  38.6 0.0 copy-done.2
  38.6 0.0 copy-start.4
  38.6 0.1 copy.38
  38.7 183.3 %all-to-all-done = bf16[16,56,7168]{2,1,0:T(8,128)(2,1)} async-done(((bf16[16,56,7168]{2,1,0:T(8,128)(2,1)}), bf16[16,56,7168]{2,1,0:T(8,128)(2,1)}, u32[]{:S(2)}, u32[]{:S(2)}) %all-to-all-start) | async-done | bytes 12845088 | tf_op jit(solution)/shard_map/all_to_all | solution.py:45
  222.0 2.1 broadcast_in_dim.94
  224.1 11.6 %all-to-all-start.1 = ((bf16[64,256,112]{1,2,0:T(8,128)(2,1)}), bf16[64,256,112]{1,2,0:T(8,128)(2,1)}, u32[]{:S(2)}, u32[]{:S(2)}) async-start(bf16[64,256,112]{1,2,0:T(8,128)(2,1)} %bitcast.78), calls=%async_computation.1 | async-start | bytes 7340032 | tf_op jit(solution)/shard_map/all_to_all | solution.py:57
  236.4 0.0 copy-done.3
  236.4 0.1 fusion.40
  236.5 0.2 copy.27
  237.3 0.2 copy.28
  237.6 0.0 copy-done.4
  237.6 0.2 and_reduce_fusion
  237.8 0.1 fusion.22
  237.9 0.0 all-gather.2.cloned.1.call-done
  237.9 6.6 %fusion.39 = (bf16[1,2048,896]{2,1,0:T(8,128)(2,1)}, bf16[1,2048,896]{2,1,0:T(8,128)(2,1)}) fusion(bf16[2,2048,896]{2,1,0:T(8,128)(2,1)} %all-gather.2.cloned.1.call-done), kind=kLoop, calls=%fused_computation.68 | loop fusion | bytes 14680064 | tf_op jit(solution)/shard_map/slice | solution.py:88
  244.5 6.1 %copy.31 = bf16[1,2048,896]{1,2,0:T(8,128)(2,1)} copy(bf16[1,2048,896]{2,1,0:T(8,128)(2,1)} %get-tuple-element.11) | data formatting | bytes 7340032 | tf_op jit(solution)/shard_map/slice | solution.py:89
  250.7 6.2 %copy.30 = bf16[1,2048,896]{1,2,0:T(8,128)(2,1)} copy(bf16[1,2048,896]{2,1,0:T(8,128)(2,1)} %get-tuple-element.10) | data formatting | bytes 7340032 | tf_op jit(solution)/shard_map/slice | solution.py:88
  256.8 1.6 constant_dynamic-slice_fusion
  258.5 1.2 copy.32
  259.7 60.8 %all-to-all-done.1 = bf16[64,256,112]{1,2,0:T(8,128)(2,1)} async-done(((bf16[64,256,112]{1,2,0:T(8,128)(2,1)}), bf16[64,256,112]{1,2,0:T(8,128)(2,1)}, u32[]{:S(2)}, u32[]{:S(2)}) %all-to-all-start.1) | async-done | bytes 3670048 | tf_op jit(solution)/shard_map/all_to_all | solution.py:57
  320.6 0.0 copy-start
  320.6 9.3 %convolution_convert_fusion = bf16[896,256]{1,0:T(8,128)(2,1)S(1)} fusion(bf16[896,7168]{1,0:T(8,128)(2,1)} %bitcast.6, bf16[256,7168]{0,1:T(8,128)(2,1)} %bitcast.10), kind=kOutput, calls=%fused_computation.17 | convolution fusion | flops 3288563712 | bytes 16973824 | tf_op jit(solution)/shard_map/td,hd->th/dot_general | solution.py:59
  329.9 0.0 copy-done
  329.9 0.0 copy-start.1
  329.9 1.9 fusion
  331.8 0.4 fusion.41
  332.2 2.2 fusion.1
  334.4 0.0 copy-done.1
  334.4 2.1 fusion.7
  336.5 0.2 fusion.16
  336.7 0.4 fusion.15
  337.2 1.0 copy.33
  (8 shorter events, 0.1 us)
Async XLA Ops:
  8.2 9.2 %collective-permute-start.2 = (bf16[56,1792]{1,0:T(8,128)(2,1)S(1)}, bf16[56,1792]{1,0:T(8,128)(2,1)S(1)}, u32[]{:S(2)}, u32[]{:S(2)}) collective-permute-start(bf16[56,1792]{1,0:T(8,128)(2,1)S(1)} %convert_element_type.21), channel_id=1, source_target_pairs={{0,192},{64,0},{128,64},{192,128},{1,193},{65,1},{129,65},{193,129... | collective-permute-start | bytes 602120 | tf_op jit(solution)/shard_map/ppermute | solution.py:38
  11.6 7.1 %collective-permute-start.1 = (bf16[56,1792]{1,0:T(8,128)(2,1)S(1)}, bf16[56,1792]{1,0:T(8,128)(2,1)S(1)}, u32[]{:S(2)}, u32[]{:S(2)}) collective-permute-start(bf16[56,1792]{1,0:T(8,128)(2,1)S(1)} %convert_element_type.21), channel_id=1, source_target_pairs={{0,128},{64,192},{128,0},{192,64},{1,129},{65,193},{129,1},{193,65... | collective-permute-start | bytes 602120 | tf_op jit(solution)/shard_map/ppermute | solution.py:38
  12.1 12.2 %collective-permute-start = (bf16[56,1792]{1,0:T(8,128)(2,1)S(1)}, bf16[56,1792]{1,0:T(8,128)(2,1)S(1)}, u32[]{:S(2)}, u32[]{:S(2)}) collective-permute-start(bf16[56,1792]{1,0:T(8,128)(2,1)S(1)} %convert_element_type.21), channel_id=1, source_target_pairs={{0,64},{64,128},{128,192},{192,0},{1,65},{65,129},{129,193},{193,1... | collective-permute-start | bytes 602120 | tf_op jit(solution)/shard_map/ppermute | solution.py:38
  31.4 7.2 %copy-start.2 = (bf16[4096,112]{0,1:T(8,128)(2,1)S(1)}, bf16[4096,112]{0,1:T(8,128)(2,1)}, u32[]{:S(2)}) copy-start(bf16[4096,112]{0,1:T(8,128)(2,1)} %param.7) | copy-start | bytes 2752516
  31.4 190.6 %all-to-all-start = ((bf16[16,56,7168]{2,1,0:T(8,128)(2,1)}), bf16[16,56,7168]{2,1,0:T(8,128)(2,1)}, u32[]{:S(2)}, u32[]{:S(2)}) async-start(bf16[16,56,7168]{2,1,0:T(8,128)(2,1)} %stack.23), calls=%async_computation | async-start | bytes 25690112 | tf_op jit(solution)/shard_map/all_to_all | solution.py:45
  37.9 198.5 %copy-start.3 = (bf16[2,256,896]{2,1,0:T(8,128)(2,1)S(1)}, bf16[2,256,896]{2,1,0:T(8,128)(2,1)}, u32[]{:S(2)}) copy-start(bf16[2,256,896]{2,1,0:T(8,128)(2,1)} %param.10) | copy-start | bytes 2752516
  37.9 200.0 %all-gather.2.cloned.1.call-start = ((), (), s32[]{:S(2)}) async-start(), calls=%async_computation.2 | async-start | bytes 7798784 | tf_op jit(solution)/shard_map/all_gather | solution.py:80
  38.6 199.0 %copy-start.4 = (s32[1,64]{1,0:T(1,128)S(1)}, s32[1,64]{1,0:T(1,128)}, u32[]{:S(2)}) copy-start(s32[1,64]{1,0:T(1,128)} %param.11) | copy-start | bytes 772
  224.1 96.5 %all-to-all-start.1 = ((bf16[64,256,112]{1,2,0:T(8,128)(2,1)}), bf16[64,256,112]{1,2,0:T(8,128)(2,1)}, u32[]{:S(2)}, u32[]{:S(2)}) async-start(bf16[64,256,112]{1,2,0:T(8,128)(2,1)} %bitcast.78), calls=%async_computation.1 | async-start | bytes 7340032 | tf_op jit(solution)/shard_map/all_to_all | solution.py:57
  320.6 9.3 %copy-start = (bf16[1,2048,896]{1,2,0:T(8,128)(2,1)S(1)}, bf16[1,2048,896]{1,2,0:T(8,128)(2,1)}, u32[]{:S(2)}) copy-start(bf16[1,2048,896]{1,2,0:T(8,128)(2,1)} %copy.30) | copy-start | bytes 11010052
  329.9 4.5 %copy-start.1 = (bf16[1,2048,896]{1,2,0:T(8,128)(2,1)S(1)}, bf16[1,2048,896]{1,2,0:T(8,128)(2,1)}, u32[]{:S(2)}) copy-start(bf16[1,2048,896]{1,2,0:T(8,128)(2,1)} %copy.31) | copy-start | bytes 11010052
Sparse Core Ops, SparseCore 0:
  40.5 177.9 all-gather.1
